TPU v7x, 32 devices: a whole 2x2x4 slice. The times are simulated.
32 devices in a mesh: dp: 16 (over z, y, x), ctx: 2 (over core).
Axes of the slice: x: 2, y: 2, z: 4, core: 2. Of those that a mesh axis runs over, the one named last changes fastest.
Arguments:
- layer_in: bfloat16 [16, 256, 4096], P('dp', 'ctx'), may hold values from -6 to 6
- inner_act: bfloat16 [16, 256, 2176], P('dp', 'ctx'), may hold values from -6 to 6
- readout: bfloat16 [16, 256, 64], P('dp', 'ctx'), may hold values from -0.75 to 0.75
- w_in: bfloat16 [4096, 132], P('dp'), may hold values from -0.09375 to 0.09375
- a_log: float32 [68], replicated, may hold values from -3.9 to -1.6
- dt_bias: float32 [68], replicated, may hold values from -4 to -1
- d_skip: float32 [68], replicated, may hold values from 0.5 to 1.5
- grad_out: bfloat16 [16, 256, 2176], P('dp', 'ctx'), may hold values from -6 to 6
Outputs:
- grad_x: bfloat16 [16, 256, 2176], P('dp', 'ctx')
- grad_c: bfloat16 [16, 256, 64], P('dp', 'ctx')
- grad_proj: bfloat16 [16, 256, 132], P('dp', 'ctx')
- grad_w: float32 [4096, 132], P('dp', 'ctx')
All inputs are finite; a program needn't handle non-finite values.
Results may differ from a plain program's by a relative error of at most 0.015.
Values may be sent and summed in bfloat16 or wider, within the bound.
A program may use at most 64 MiB of HBM per device.

v0:
```python
import jax
import jax.numpy as jnp
from jax import lax
from jax.sharding import PartitionSpec as P

STATE = 64
BLOCK = 128


def entering(array, axis, join, neutral, backward):
    count = lax.axis_size(axis)
    place = lax.axis_index(axis)
    ahead = count - 1 - place if backward else place
    gathered = jax.tree.map(
        lambda a, kind: lax.all_gather(a.astype(kind), axis), array, (jnp.bfloat16, jnp.bfloat16)
    )
    state = jax.tree.map(lambda a, e: jnp.zeros_like(a) + jnp.asarray(e, a.dtype), array, neutral)

    def one(turn, state):
        source = count - 1 - turn if backward else turn
        return join(
            state,
            jax.tree.map(
                lambda a, own: lax.dynamic_index_in_dim(a, source, 0, False).astype(own.dtype),
                gathered,
                array,
            ),
        )

    return lax.fori_loop(0, ahead, one, state)


def prepare(projected, a_log, dt_bias):
    b_rows = projected[:, :STATE].astype(jnp.bfloat16)
    step_size = jax.nn.softplus(projected[:, STATE:] + dt_bias)
    decay_rate = -jnp.exp(a_log) * step_size
    return (b_rows, step_size, decay_rate)


def blocked(values, width):
    return values.reshape(values.shape[0] // BLOCK, BLOCK, width)


def split_blocks(projected, inner_rows, a_log, dt_bias):
    row_count = projected.shape[0]
    head_count = a_log.shape[0]
    head_width = inner_rows.shape[1] // head_count
    b_rows, step_size, decay_rate = prepare(projected, a_log, dt_bias)
    inner_blocks = inner_rows.reshape(row_count // BLOCK, BLOCK, head_count, head_width)
    step_blocks = jnp.swapaxes(blocked(step_size, head_count), 1, 2)
    cum_blocks = jnp.cumsum(jnp.swapaxes(blocked(decay_rate, head_count), 1, 2), axis=2)
    return (inner_blocks, blocked(b_rows, STATE), step_blocks, cum_blocks, decay_rate)


def state_input(inner_c, b_c, step_c, cum_c):
    to_end = jnp.exp(cum_c[:, -1:] - cum_c) * step_c
    weighted = (b_c.astype(jnp.float32)[None] * to_end[:, :, None]).astype(jnp.bfloat16)
    return jnp.einsum("shp,hsn->hpn", inner_c, weighted, preferred_element_type=jnp.float32)


def block_forward(projected, inner_rows, c_rows, a_log, dt_bias, d_skip, entry_state):
    row_count = projected.shape[0]
    inner_blocks, b_blocks, step_blocks, cum_blocks, decay_rate = split_blocks(
        projected, inner_rows, a_log, dt_bias
    )
    c_blocks = blocked(c_rows, STATE)
    position = jnp.arange(BLOCK)
    causal = position[:, None] >= position[None, :]

    def block_advance(carried, pieces):
        inner_c, b_c, c_c, step_c, cum_c = pieces
        scores = jnp.dot(c_c, b_c.T, preferred_element_type=jnp.float32)
        spread = cum_c[:, :, None] - cum_c[:, None, :]
        factor = jnp.where(causal, jnp.exp(jnp.where(causal, spread, 0.0)), 0.0)
        mixing = (scores[None] * factor * step_c[:, None, :]).astype(jnp.bfloat16)
        within = jnp.einsum("hts,shp->thp", mixing, inner_c, preferred_element_type=jnp.float32)
        added = state_input(inner_c, b_c, step_c, cum_c)
        carried_in = jnp.einsum(
            "tn,hpn->thp", c_c.astype(jnp.float32), carried, precision=lax.Precision.HIGHEST
        )
        carried_in = carried_in * jnp.exp(cum_c).T[:, :, None]
        result = (within + carried_in + d_skip[None, :, None] * inner_c.astype(jnp.float32)).astype(
            jnp.bfloat16
        )
        carried = jnp.exp(cum_c[:, -1])[:, None, None] * carried + added
        return (carried, result)

    final_state, outputs = lax.scan(
        block_advance, entry_state, (inner_blocks, b_blocks, c_blocks, step_blocks, cum_blocks)
    )
    return (outputs.reshape(row_count, inner_rows.shape[1]), final_state)


def local_summary(projected, inner_rows, a_log, dt_bias):
    inner_blocks, b_blocks, step_blocks, cum_blocks, decay_rate = split_blocks(
        projected, inner_rows, a_log, dt_bias
    )
    head_count = a_log.shape[0]
    head_width = inner_rows.shape[1] // head_count

    def local_advance(carried, pieces):
        inner_c, b_c, step_c, cum_c = pieces
        added = state_input(inner_c, b_c, step_c, cum_c)
        return (jnp.exp(cum_c[:, -1])[:, None, None] * carried + added, None)

    zero_state = jnp.zeros((head_count, head_width, STATE), jnp.float32)
    final_state, unused = lax.scan(
        local_advance, zero_state, (inner_blocks, b_blocks, step_blocks, cum_blocks)
    )
    return (jnp.exp(jnp.sum(decay_rate, axis=0)), final_state)


def entry_weights(projected, c_rows, grad_rows, a_log, dt_bias):
    b_rows, step_size, decay_rate = prepare(projected, a_log, dt_bias)
    row_count = projected.shape[0]
    head_count = a_log.shape[0]
    head_width = grad_rows.shape[1] // head_count
    growth = jnp.exp(jnp.cumsum(decay_rate, axis=0))
    weighted = (c_rows.astype(jnp.float32)[:, None, :] * growth[:, :, None]).astype(jnp.bfloat16)
    return jnp.einsum(
        "thp,thn->hpn",
        grad_rows.reshape(row_count, head_count, head_width),
        weighted,
        preferred_element_type=jnp.float32,
    )


def combine_carry(earlier, later):
    return (earlier[0] * later[0], later[1] + later[0][:, None, None] * earlier[1])


def pass_along(decay_total, summary, backward):
    identity = (jnp.ones_like(decay_total), jnp.zeros_like(summary))
    return entering((decay_total, summary), "ctx", combine_carry, identity, backward)


def per_device(layer_in, inner_act, readout, w_in, a_log, dt_bias, d_skip, grad_out):
    tokens = layer_in[0]
    inner_rows = inner_act[0]
    c_rows = readout[0]
    grad_rows = grad_out[0]
    w_full = lax.all_gather(w_in, "dp", axis=0, tiled=True)
    projected = jnp.dot(tokens, w_full, preferred_element_type=jnp.float32)
    decay_total, own_state = local_summary(projected, inner_rows, a_log, dt_bias)
    entry_part = entry_weights(projected, c_rows, grad_rows, a_log, dt_bias)
    entry_state = pass_along(decay_total, own_state, False)[1]
    exit_grad = pass_along(decay_total, entry_part, True)[1]

    def recompute(proj_val, inner_val, c_val):
        return block_forward(proj_val, inner_val, c_val, a_log, dt_bias, d_skip, entry_state)

    primal, pullback = jax.vjp(recompute, projected, inner_rows, c_rows)
    grad_p, grad_v, grad_r = pullback((grad_rows, exit_grad))
    proj_grad = grad_p.astype(jnp.bfloat16)
    seq_count = lax.axis_size("dp")
    contract = (((0,), (0,)), ((), ()))
    summed = lax.psum_scatter(
        lax.dot_general(tokens, proj_grad, contract, preferred_element_type=jnp.float32),
        "dp",
        scatter_dimension=0,
        tiled=True,
    )
    weight_grad = lax.psum_scatter(summed, "ctx", scatter_dimension=1, tiled=True)
    return (grad_v[None], grad_r[None], proj_grad[None], weight_grad / seq_count)


def solution(mesh):
    in_specs = (
        P("dp", "ctx", None),
        P("dp", "ctx", None),
        P("dp", "ctx", None),
        P("dp", None),
        P(),
        P(),
        P(),
        P("dp", "ctx", None),
    )
    out_specs = (P("dp", "ctx", None), P("dp", "ctx", None), P("dp", "ctx", None), P("dp", "ctx"))
    return jax.shard_map(
        per_device, mesh=mesh, in_specs=in_specs, out_specs=out_specs, check_vma=False
    )
```

profile of v0, /device:TPU:0, one launch (start us, length us, event | category | flops | bytes accessed | tf_op | source)
XLA Modules:
  0.0 213.8 jit_solution(7782846302152594224)
XLA Ops:
  8.0 1.4 copy.64
  9.4 1.1 copy.76
  12.5 56.9 %all-gather.5.cloned.1.call-done = bf16[4096,132]{0,1:T(8,128)(2,1)} async-done(((bf16[256,132]{0,1:T(8,128)(2,1)}), bf16[4096,132]{0,1:T(8,128)(2,1)}) %all-gather.5.cloned.1.call-update) | async-done | bytes 1081360 | tf_op jit(solution)/shard_map/all_gather | solution.py:142
  69.4 1.7 fusion.46
  74.6 2.6 %all-gather = bf16[136,32,64]{2,1,0:T(8,128)(2,1)S(1)} all-gather(bf16[68,32,64]{2,1,0:T(8,128)(2,1)S(1)} %fusion.29), channel_id=2, replica_groups=mesh['dp'=16,'ctx'=2] {'ctx'}, dimensions={0}, use_global_device_ids=true | all-gather | bytes 835584 | tf_op jit(solution)/shard_map/all_gather | solution.py:15
  77.5 2.4 %all-reduce.4 = bf16[136]{0:T(256)(128)(2,1)S(1)} all-reduce(bf16[136]{0:T(256)(128)(2,1)S(1)} %dynamic-update-slice), channel_id=3, replica_groups=mesh['dp'=16,'ctx'=2] {'ctx'}, use_global_device_ids=true, to_apply=%add.4 | all-reduce | flops 136 | bytes 544
  80.5 2.4 %fusion.13 = (f32[68,128]{1,0:T(8,128)}, bf16[128,64]{0,1:T(8,128)(2,1)}) fusion(f32[128,64]{0,1:T(8,128)} %fusion.68, f32[68,128]{1,0:T(8,128)} %copy.69, f32[68,32,64]{2,1,0:T(8,128)S(1)} %get-tuple-element.513, bf16[128,68,32]{0,2,1:T(8,128)(2,1)} %bitcast.174), kind=kOutput, calls=%fused_computation.23 | convolution fusion | flops 38419968 | bytes 1232896 | tf_op jit(solution)/shard_map/transpose(jvp())/while/body/eval_jaxpr/shp,hsn->hpn/dot_general | solution.py:58
  83.6 2.7 %all-gather.2 = bf16[136,32,64]{2,1,0:T(8,128)(2,1)} all-gather(bf16[68,32,64]{2,1,0:T(8,128)(2,1)S(1)} %fusion.28), channel_id=4, replica_groups=mesh['dp'=16,'ctx'=2] {'ctx'}, dimensions={0}, use_global_device_ids=true | all-gather | bytes 835584 | tf_op jit(solution)/shard_map/all_gather | solution.py:15
  87.7 1.3 fusion.27
  89.9 0.9 copy.78
  92.7 1.5 copy.80
  94.2 1.6 copy.70
  95.7 6.0 %fusion.11 = (f32[68,128]{1,0:T(8,128)}, f32[68,128]{1,0:T(8,128)}, f32[68,128]{1,0:T(8,128)}, bf16[128,128]{1,0:T(8,128)(2,1)}) fusion(f32[68,128]{1,0:T(8,128)} %copy.73, f32[68,128]{1,0:T(8,128)} %bitcast.177, f32[128,128]{1,0:T(8,128)} %copy.70, pred[128,128]{1,0:T(8,128)(4,1)} %iota_compare_fusion, bf16[68,32,128]{2,1,0:T(8,128)(2,1)} %bitcast.164, ...), kind=kOutput, calls=%fused_computation.19 | convolution fusion | flops 90200576 | bytes 1402880 | tf_op jit(solution)/shard_map/transpose(jvp())/while/body/eval_jaxpr/hts,shp->thp/dot_general | solution.py:76
  101.7 1.5 copy.82
  103.2 1.5 copy.83
  104.7 1.6 fusion.57
  106.2 0.9 copy.84
  107.2 1.9 reduce_window_sum.37
  109.0 1.5 copy.85
  110.5 1.5 copy.79
  112.0 1.4 copy.86
  113.4 1.0 fusion.50
  114.4 1.0 fusion.41
  115.4 1.9 convolution_bitcast_fusion
  118.2 1.1 bitcast_multiply_fusion.2
  119.4 2.0 fusion.42
  121.4 1.5 fusion.44
  123.0 2.0 fusion.30
  125.5 72.9 %reduce-scatter.4.cloned.1.call-done = f32[256,132]{0,1:T(8,128)} async-done(((f32[4096,132]{0,1:T(8,128)}), f32[256,132]{0,1:T(8,128)}) %reduce-scatter.4.cloned.1.call-update) | async-done | bytes 135184 | tf_op jit(solution)/shard_map/reduce_scatter | solution.py:157
  198.4 3.6 %fusion = f32[256,72]{0,1:T(8,128)S(1)} fusion(f32[256,132]{0,1:T(8,128)} %reduce-scatter.4.cloned.1.call-done), kind=kCustom, calls=%all-reduce-scatter | all-reduce-scatter fusion | flops 36865 | bytes 209408
  202.0 2.3 %collective-permute-start = (f32[256,6]{0,1:T(8,128)S(1)}, f32[256,6]{0,1:T(8,128)S(1)}, u32[]{:S(2)}, u32[]{:S(2)}) collective-permute-start(f32[256,6]{0,1:T(8,128)S(1)} %slice.28), channel_id=1, source_target_pairs={{0,1},{2,3},{4,5},{6,7},{8,9},{10,11},{12,13},{14,15},{16,17},{18,... | collective-permute-start | bytes 18440
  205.1 1.1 copy.88
  (101 shorter events, 13.7 us)
Async XLA Ops:
  7.2 62.2 %copy-start = (bf16[1,128,4096]{2,1,0:T(8,128)(2,1)S(1)}, bf16[1,128,4096]{2,1,0:T(8,128)(2,1)}, u32[]{:S(2)}) copy-start(bf16[1,128,4096]{2,1,0:T(8,128)(2,1)} %param.12) | copy-start | bytes 3145732
  7.2 2.2 %copy-start.4 = (bf16[1,128,2176]{2,1,0:T(8,128)(2,1)S(1)}, bf16[1,128,2176]{2,1,0:T(8,128)(2,1)}, u32[]{:S(2)}) copy-start(bf16[1,128,2176]{2,1,0:T(8,128)(2,1)} %param.13) | copy-start | bytes 1671172
  7.2 62.2 %all-gather.5.cloned.1.call-start = ((), (), s32[]{:S(2)}) async-start(), calls=%async_computation.1 | async-start | bytes 1183744 | tf_op jit(solution)/shard_map/all_gather | solution.py:142
  7.9 190.4 %reduce-scatter.4.cloned.1.call-start = ((), (), s32[]{:S(2)}) async-start(), calls=%async_computation.2 | async-start | bytes 2367488 | tf_op jit(solution)/shard_map/reduce_scatter | solution.py:157
  8.0 2.5 %copy-start.24 = (u32[32]{0:T(128)S(1)}, u32[32]{0:T(128)}, u32[]{:S(2)}) copy-start(u32[32]{0:T(128)} %constant.223) | copy-start | bytes 388
  8.0 4.4 %copy-start.26 = (f32[68]{0:T(128)S(1)}, f32[68]{0:T(128)}, u32[]{:S(2)}) copy-start(f32[68]{0:T(128)} %param.16) | copy-start | bytes 820
  8.0 4.4 %copy-start.7 = (bf16[1,128,64]{1,2,0:T(8,128)(2,1)S(1)}, bf16[1,128,64]{1,2,0:T(8,128)(2,1)}, u32[]{:S(2)}) copy-start(bf16[1,128,64]{1,2,0:T(8,128)(2,1)} %param.14) | copy-start | bytes 49156
  9.4 64.6 %copy-start.1 = (bf16[1,128,2176]{1,2,0:T(8,128)(2,1)}, bf16[1,128,2176]{1,2,0:T(8,128)(2,1)S(1)}, u32[]{:S(2)}) copy-start(bf16[1,128,2176]{1,2,0:T(8,128)(2,1)S(1)} %copy.64) | copy-start | bytes 1671172
  12.4 59.4 %copy-start.23 = (f32[68]{0:T(128)}, f32[68]{0:T(128)S(1)}, u32[]{:S(2)}) copy-start(f32[68]{0:T(128)S(1)} %exponential_negate_fusion) | copy-start | bytes 820
  12.4 59.4 %copy-start.22 = (f32[68]{0:T(128)S(1)}, f32[68]{0:T(128)}, u32[]{:S(2)}) copy-start(f32[68]{0:T(128)} %param.17) | copy-start | bytes 820
  71.1 18.0 %copy-start.6 = (f32[128,132]{0,1:T(8,128)}, f32[128,132]{0,1:T(8,128)S(1)}, u32[]{:S(2)}) copy-start(f32[128,132]{0,1:T(8,128)S(1)} %fusion.46) | copy-start | bytes 202756
  72.3 0.6 copy-start.11
  72.9 18.6 %copy-start.21 = (f32[68]{0:T(128)}, f32[68]{0:T(128)S(1)}, u32[]{:S(2)}) copy-start(f32[68]{0:T(128)S(1)} %slice_bitcast_fusion) | copy-start | bytes 820
  80.5 2.4 %copy-start.5 = (bf16[1,128,2176]{1,2,0:T(8,128)(2,1)S(1)}, bf16[1,128,2176]{1,2,0:T(8,128)(2,1)}, u32[]{:S(2)}) copy-start(bf16[1,128,2176]{1,2,0:T(8,128)(2,1)} %copy.76) | copy-start | bytes 1671172
  80.5 2.4 %copy-start.13 = (f32[68,128]{1,0:T(8,128)S(1)}, f32[68,128]{1,0:T(8,128)}, u32[]{:S(2)}) copy-start(f32[68,128]{1,0:T(8,128)} %copy.69) | copy-start | bytes 104452
  80.5 2.4 %copy-start.15 = (f32[128,64]{0,1:T(8,128)S(1)}, f32[128,64]{0,1:T(8,128)}, u32[]{:S(2)}) copy-start(f32[128,64]{0,1:T(8,128)} %fusion.68) | copy-start | bytes 98308
  86.7 1.1 copy-start.2
  86.7 1.0 copy-start.8
  101.7 12.7 %copy-start.9 = (bf16[1,128,64]{1,2,0:T(8,128)(2,1)S(1)}, bf16[1,128,64]{1,2,0:T(8,128)(2,1)}, u32[]{:S(2)}) copy-start(bf16[1,128,64]{1,2,0:T(8,128)(2,1)} %param.14) | copy-start | bytes 49156
  117.3 0.8 copy-start.10
  119.4 2.0 copy-start.17
  119.4 3.6 %copy-start.3 = (bf16[1,128,2176]{1,2,0:T(8,128)(2,1)S(1)}, bf16[1,128,2176]{1,2,0:T(8,128)(2,1)}, u32[]{:S(2)}) copy-start(bf16[1,128,2176]{1,2,0:T(8,128)(2,1)} %copy-done.1) | copy-start | bytes 1671172
  119.4 3.5 %copy-start.12 = (f32[1,68,128]{2,1,0:T(8,128)S(1)}, f32[1,68,128]{2,1,0:T(8,128)}, u32[]{:S(2)}) copy-start(f32[1,68,128]{2,1,0:T(8,128)} %copy-done.11) | copy-start | bytes 104452
  119.4 3.5 %copy-start.18 = (f32[128,128]{1,0:T(8,128)S(1)}, f32[128,128]{1,0:T(8,128)}, u32[]{:S(2)}) copy-start(f32[128,128]{1,0:T(8,128)} %copy.70) | copy-start | bytes 196612
  119.4 3.5 %copy-start.19 = (f32[68,128]{1,0:T(8,128)S(1)}, f32[68,128]{1,0:T(8,128)}, u32[]{:S(2)}) copy-start(f32[68,128]{1,0:T(8,128)} %copy.73) | copy-start | bytes 104452
  119.4 3.5 %copy-start.20 = (pred[128,128]{1,0:T(8,128)(4,1)S(1)}, pred[128,128]{1,0:T(8,128)(4,1)}, u32[]{:S(2)}) copy-start(pred[128,128]{1,0:T(8,128)(4,1)} %iota_compare_fusion) | copy-start | bytes 49156
  123.0 2.0 copy-start.14
  123.0 2.0 copy-start.16
  123.0 2.0 copy-start.25
  202.0 4.1 %collective-permute-start = (f32[256,6]{0,1:T(8,128)S(1)}, f32[256,6]{0,1:T(8,128)S(1)}, u32[]{:S(2)}, u32[]{:S(2)}) collective-permute-start(f32[256,6]{0,1:T(8,128)S(1)} %slice.28), channel_id=1, source_target_pairs={{0,1},{2,3},{4,5},{6,7},{8,9},{10,11},{12,13},{14,15},{16,17},{18,... | collective-permute-start | bytes 18440
Sparse Core Ops, SparseCore 0:
  10.7 58.5 all-gather.4
  117.5 80.8 reduce-scatter.3
where the time goes:
time: 215 us; the launch traced here: 214 us
  waiting for transfers between devices  130 us (60%)
  matrix products  22.4 us (10%)
  local copies, waits for them, and re-layouts  20.8 us (10%)
  between operations  15.9 us (7%)
  blocking collectives  11.4 us (5%)
  other arithmetic  10.2 us (5%)
  starting transfers between devices  2.33 us (1%)
    reduce_scatter x1, waiting for transfers between devices, per_device(): lax.psum_scatter(lax.dot_general(tokens, proj_grad, contract, preferred_e...  72.9 us
    all_gather x1, waiting for transfers between devices, per_device(): w_full = lax.all_gather(w_in, 'dp', axis=0, tiled=True)  56.9 us
    dot_general x2, matrix products, block_advance(): jnp.einsum('hts,shp->thp', mixing, inner_c, preferred_element_type=jnp.fl...  7.92 us
    unnamed x64, local copies, waits for them, and re-layouts  6.5 us
    unnamed x2, blocking collectives  6.08 us
    all_gather x2, blocking collectives, entering(): lax.all_gather(a.astype(kind), axis)  5.35 us
  transfers between devices with their start and end apart: 3, of which 2 were waited for; matrix products, arithmetic and copies ran while one was open for 6% of the time, Pallas kernels for 0%

commit v1 on v0

--- a/solution.py
+++ b/solution.py
@@ -139,7 +139,14 @@
     inner_rows = inner_act[0]
     c_rows = readout[0]
     grad_rows = grad_out[0]
-    w_full = lax.all_gather(w_in, "dp", axis=0, tiled=True)
+    finding, part_next = (lax.axis_size("dp"), lax.axis_index("dp"))
+    w_full, prior = (w_in, 1)
+    while prior < finding:
+        t_next = lax.ppermute(w_full, "dp", [(t, t ^ prior) for t in range(finding)])
+        m_next = jnp.concatenate([w_full, t_next], 0)
+        tmp = jnp.concatenate([t_next, w_full], 0)
+        w_full = jnp.where(part_next & prior == 0, m_next, tmp)
+        prior = 2 * prior
     projected = jnp.dot(tokens, w_full, preferred_element_type=jnp.float32)
     decay_total, own_state = local_summary(projected, inner_rows, a_log, dt_bias)
     entry_part = entry_weights(projected, c_rows, grad_rows, a_log, dt_bias)

time: 215 us -> 201 us (0.935)
  waiting for transfers between devices: 130 us -> 100 us
  starting transfers between devices: 2.33 us -> 13.5 us
  other arithmetic: 10.2 us -> 14.8 us
    all_gather x1 -> x0, waiting for transfers between devices: 56.9 us -> none  [per_device(): w_full = lax.all_gather(w_in, 'dp', axis=0, tiled=True)]
    ppermute x0 -> x4, waiting for transfers between devices: none -> 26.3 us  [per_device(): lax.ppermute(w_full, 'dp', [(t, t ^ prior) for t in range(finding)])]
    ppermute x0 -> x4, starting transfers between devices: none -> 11.2 us  [per_device(): lax.ppermute(w_full, 'dp', [(t, t ^ prior) for t in range(finding)])]
    unnamed x64 -> x65, local copies, waits for them, and re-layouts: 6.5 us -> 5.34 us
  transfers between devices with their start and end apart: 3 -> 6, of which waited for: 2 -> 5; matrix products, arithmetic and copies ran while one was open for 6% -> 6% of each run, Pallas kernels for 0% -> 0%
where the time goes in v1:
time: 201 us; the launch traced here: 200 us
  waiting for transfers between devices  100 us (50%)
  local copies, waits for them, and re-layouts  21.7 us (11%)
  matrix products  21.4 us (11%)
  between operations  15.9 us (8%)
  other arithmetic  14.8 us (7%)
  starting transfers between devices  13.5 us (7%)
  blocking collectives  12.1 us (6%)
    reduce_scatter x1, waiting for transfers between devices, per_device(): lax.psum_scatter(lax.dot_general(tokens, proj_grad, contract, preferred_e...  74 us
    ppermute x4, waiting for transfers between devices, per_device(): lax.ppermute(w_full, 'dp', [(t, t ^ prior) for t in range(finding)])  26.3 us
    ppermute x4, starting transfers between devices, per_device(): lax.ppermute(w_full, 'dp', [(t, t ^ prior) for t in range(finding)])  11.2 us
    dot_general x2, matrix products, block_advance(): jnp.einsum('hts,shp->thp', mixing, inner_c, preferred_element_type=jnp.fl...  7.93 us
    unnamed x2, blocking collectives  6.08 us
    all_gather x2, blocking collectives, entering(): lax.all_gather(a.astype(kind), axis)  6.05 us
    unnamed x65, local copies, waits for them, and re-layouts  5.34 us
  transfers between devices with their start and end apart: 6, of which 5 were waited for; matrix products, arithmetic and copies ran while one was open for 6% of the time, Pallas kernels for 0%

profile of v1, /device:TPU:0, one launch (start us, length us, event | category | flops | bytes accessed | tf_op | source)
XLA Modules:
  0.0 200.1 jit_solution(46188397820309187)
XLA Ops:
  7.2 3.0 %collective-permute-start = (bf16[256,132]{0,1:T(8,128)(2,1)}, bf16[256,132]{0,1:T(8,128)(2,1)S(1)}, u32[]{:S(2)}, u32[]{:S(2)}) collective-permute-start(bf16[256,132]{0,1:T(8,128)(2,1)} %param.15), channel_id=1, source_target_pairs={{0,2},{2,0},{4,6},{6,4},{8,10},{10,8},{12,14},{14,12},{16,18},{18,... | collective-permute-start | bytes 202760 | tf_op jit(solution)/shard_map/ppermute | solution.py:145
  10.2 2.5 %collective-permute-done = bf16[256,132]{0,1:T(8,128)(2,1)S(1)} collective-permute-done((bf16[256,132]{0,1:T(8,128)(2,1)}, bf16[256,132]{0,1:T(8,128)(2,1)S(1)}, u32[]{:S(2)}, u32[]{:S(2)}) %collective-permute-start) | collective-permute-done | bytes 67616 | tf_op jit(solution)/shard_map/ppermute | solution.py:145
  13.7 2.1 %collective-permute-start.1 = (bf16[512,132]{0,1:T(8,128)(2,1)S(1)}, bf16[512,132]{0,1:T(8,128)(2,1)S(1)}, u32[]{:S(2)}, u32[]{:S(2)}) collective-permute-start(bf16[512,132]{0,1:T(8,128)(2,1)S(1)} %maximum_select_fusion.4), channel_id=1, source_target_pairs={{0,4},{2,6},{4,0},{6,2},{8,12},{10,14},{12,8},{14,10},{16,20},{18,... | collective-permute-start | bytes 405512 | tf_op jit(solution)/shard_map/ppermute | solution.py:145
  15.9 3.0 %collective-permute-done.1 = bf16[512,132]{0,1:T(8,128)(2,1)S(1)} collective-permute-done((bf16[512,132]{0,1:T(8,128)(2,1)S(1)}, bf16[512,132]{0,1:T(8,128)(2,1)S(1)}, u32[]{:S(2)}, u32[]{:S(2)}) %collective-permute-start.1) | collective-permute-done | bytes 135200 | tf_op jit(solution)/shard_map/ppermute | solution.py:145
  19.0 2.1 %collective-permute-start.2 = (bf16[1024,132]{0,1:T(8,128)(2,1)S(1)}, bf16[1024,132]{0,1:T(8,128)(2,1)S(1)}, u32[]{:S(2)}, u32[]{:S(2)}) collective-permute-start(bf16[1024,132]{0,1:T(8,128)(2,1)S(1)} %maximum_select_fusion.3), channel_id=1, source_target_pairs={{0,8},{2,10},{4,12},{6,14},{8,0},{10,2},{12,4},{14,6},{16,24},{18,... | collective-permute-start | bytes 811016 | tf_op jit(solution)/shard_map/ppermute | solution.py:145
  23.9 1.8 collective-permute-done.2
  25.8 4.0 %collective-permute-start.3 = (bf16[2048,132]{0,1:T(8,128)(2,1)S(1)}, bf16[2048,132]{0,1:T(8,128)(2,1)S(1)}, u32[]{:S(2)}, u32[]{:S(2)}) collective-permute-start(bf16[2048,132]{0,1:T(8,128)(2,1)S(1)} %maximum_select_fusion.2), channel_id=1, source_target_pairs={{0,16},{2,18},{4,20},{6,22},{8,24},{10,26},{12,28},{14,30},{16,0},... | collective-permute-start | bytes 1622024 | tf_op jit(solution)/shard_map/ppermute | solution.py:145
  31.0 19.0 %collective-permute-done.3 = bf16[2048,132]{0,1:T(8,128)(2,1)S(1)} collective-permute-done((bf16[2048,132]{0,1:T(8,128)(2,1)S(1)}, bf16[2048,132]{0,1:T(8,128)(2,1)S(1)}, u32[]{:S(2)}, u32[]{:S(2)}) %collective-permute-start.3) | collective-permute-done | bytes 540704 | tf_op jit(solution)/shard_map/ppermute | solution.py:145
  53.3 2.6 %all-gather.2 = bf16[136,32,64]{2,1,0:T(8,128)(2,1)S(1)} all-gather(bf16[68,32,64]{2,1,0:T(8,128)(2,1)S(1)} %fusion.28), channel_id=4, replica_groups=mesh['dp'=16,'ctx'=2] {'ctx'}, dimensions={0}, use_global_device_ids=true | all-gather | bytes 835584 | tf_op jit(solution)/shard_map/all_gather | solution.py:15
  56.2 2.4 %all-reduce.4 = bf16[136]{0:T(256)(128)(2,1)S(1)} all-reduce(bf16[136]{0:T(256)(128)(2,1)S(1)} %dynamic-update-slice), channel_id=3, replica_groups=mesh['dp'=16,'ctx'=2] {'ctx'}, use_global_device_ids=true, to_apply=%add.4 | all-reduce | flops 136 | bytes 544
  59.7 1.8 fusion.29
  61.5 3.4 %all-gather = bf16[136,32,64]{2,1,0:T(8,128)(2,1)} all-gather(bf16[68,32,64]{2,1,0:T(8,128)(2,1)S(1)} %fusion.29), channel_id=2, replica_groups=mesh['dp'=16,'ctx'=2] {'ctx'}, dimensions={0}, use_global_device_ids=true | all-gather | bytes 835584 | tf_op jit(solution)/shard_map/all_gather | solution.py:15
  65.1 1.5 while.20
  66.6 2.3 %fusion.13 = (f32[68,128]{1,0:T(8,128)}, bf16[128,64]{0,1:T(8,128)(2,1)}) fusion(f32[128,64]{0,1:T(8,128)} %copy-done.15, f32[68,128]{1,0:T(8,128)S(1)} %copy-done.13, f32[68,32,64]{2,1,0:T(8,128)S(1)} %get-tuple-element.513, bf16[128,68,32]{0,2,1:T(8,128)(2,1)} %bitcast.178), kind=kOutput, calls=%fused_computation.23 | convolution fusion | flops 38419968 | bytes 1232896 | tf_op jit(solution)/shard_map/transpose(jvp())/while/body/eval_jaxpr/shp,hsn->hpn/dot_general | solution.py:58
  74.8 1.5 copy.82
  76.3 1.5 copy.75
  77.9 1.6 copy.72
  79.5 6.0 %fusion.11 = (f32[68,128]{1,0:T(8,128)}, f32[68,128]{1,0:T(8,128)}, f32[68,128]{1,0:T(8,128)}, bf16[128,128]{1,0:T(8,128)(2,1)}) fusion(f32[68,128]{1,0:T(8,128)} %copy.75, f32[68,128]{1,0:T(8,128)} %bitcast.180, f32[128,128]{1,0:T(8,128)} %copy.72, pred[128,128]{1,0:T(8,128)(4,1)} %iota_compare_fusion, bf16[68,32,128]{2,1,0:T(8,128)(2,1)} %bitcast.167, ...), kind=kOutput, calls=%fused_computation.19 | convolution fusion | flops 90200576 | bytes 1402880 | tf_op jit(solution)/shard_map/transpose(jvp())/while/body/eval_jaxpr/hts,shp->thp/dot_general | solution.py:76
  85.4 1.5 copy.84
  86.9 1.5 copy.85
  88.4 1.7 fusion.62
  90.1 1.5 copy.86
  91.6 2.6 %reduce_window_sum.37 = f32[1,68,128]{2,1,0:T(8,128)} reduce-window(f32[1,68,128]{2,1,0:T(8,128)} %copy.86, f32[]{:T(128)} %constant.209.clone.1), window={size=1x1x128 pad=0_0x0_0x0_127}, to_apply=%region_15.16 | reduce-window | flops 1105408 | bytes 69636 | tf_op jit(solution)/shard_map/transpose(jvp(jit(cumsum)))/reduce_window_sum | solution.py:51
  94.2 1.5 copy.87
  95.7 1.5 copy.81
  97.2 1.4 copy.88
  100.6 1.9 convolution_bitcast_fusion
  105.3 2.0 fusion.48
  108.2 2.0 fusion.30
  110.7 74.0 %reduce-scatter.4.cloned.1.call-done = f32[256,132]{0,1:T(8,128)} async-done(((f32[4096,132]{0,1:T(8,128)}), f32[256,132]{0,1:T(8,128)}) %reduce-scatter.4.cloned.1.call-update) | async-done | bytes 135184 | tf_op jit(solution)/shard_map/reduce_scatter | solution.py:164
  184.7 3.6 %fusion = f32[256,72]{0,1:T(8,128)S(1)} fusion(f32[256,132]{0,1:T(8,128)} %reduce-scatter.4.cloned.1.call-done), kind=kCustom, calls=%all-reduce-scatter | all-reduce-scatter fusion | flops 36865 | bytes 209408
  188.3 2.3 %collective-permute-start.4 = (f32[256,6]{0,1:T(8,128)S(1)}, f32[256,6]{0,1:T(8,128)S(1)}, u32[]{:S(2)}, u32[]{:S(2)}) collective-permute-start(f32[256,6]{0,1:T(8,128)S(1)} %slice.28), channel_id=1, source_target_pairs={{0,1},{2,3},{4,5},{6,7},{8,9},{10,11},{12,13},{14,15},{16,17},{18,... | collective-permute-start | bytes 18440
  (110 shorter events, 24.3 us)
Async XLA Ops:
  7.2 42.9 %copy-start = (bf16[1,128,4096]{2,1,0:T(8,128)(2,1)S(1)}, bf16[1,128,4096]{2,1,0:T(8,128)(2,1)}, u32[]{:S(2)}) copy-start(bf16[1,128,4096]{2,1,0:T(8,128)(2,1)} %param.12) | copy-start | bytes 3145732
  7.2 14.0 %copy-start.5 = (bf16[1,128,2176]{2,1,0:T(8,128)(2,1)S(1)}, bf16[1,128,2176]{2,1,0:T(8,128)(2,1)}, u32[]{:S(2)}) copy-start(bf16[1,128,2176]{2,1,0:T(8,128)(2,1)} %param.13) | copy-start | bytes 1671172
  7.2 14.3 %copy-start.6 = (bf16[1,128,2176]{2,1,0:T(8,128)(2,1)S(1)}, bf16[1,128,2176]{2,1,0:T(8,128)(2,1)}, u32[]{:S(2)}) copy-start(bf16[1,128,2176]{2,1,0:T(8,128)(2,1)} %param.19) | copy-start | bytes 1671172
  7.2 177.5 %reduce-scatter.4.cloned.1.call-start = ((), (), s32[]{:S(2)}) async-start(), calls=%async_computation.1 | async-start | bytes 2367488 | tf_op jit(solution)/shard_map/reduce_scatter | solution.py:164
  7.2 5.5 %collective-permute-start = (bf16[256,132]{0,1:T(8,128)(2,1)}, bf16[256,132]{0,1:T(8,128)(2,1)S(1)}, u32[]{:S(2)}, u32[]{:S(2)}) collective-permute-start(bf16[256,132]{0,1:T(8,128)(2,1)} %param.15), channel_id=1, source_target_pairs={{0,2},{2,0},{4,6},{6,4},{8,10},{10,8},{12,14},{14,12},{16,18},{18,... | collective-permute-start | bytes 202760 | tf_op jit(solution)/shard_map/ppermute | solution.py:145
  13.7 5.2 %collective-permute-start.1 = (bf16[512,132]{0,1:T(8,128)(2,1)S(1)}, bf16[512,132]{0,1:T(8,128)(2,1)S(1)}, u32[]{:S(2)}, u32[]{:S(2)}) collective-permute-start(bf16[512,132]{0,1:T(8,128)(2,1)S(1)} %maximum_select_fusion.4), channel_id=1, source_target_pairs={{0,4},{2,6},{4,0},{6,2},{8,12},{10,14},{12,8},{14,10},{16,20},{18,... | collective-permute-start | bytes 405512 | tf_op jit(solution)/shard_map/ppermute | solution.py:145
  19.0 6.7 %collective-permute-start.2 = (bf16[1024,132]{0,1:T(8,128)(2,1)S(1)}, bf16[1024,132]{0,1:T(8,128)(2,1)S(1)}, u32[]{:S(2)}, u32[]{:S(2)}) collective-permute-start(bf16[1024,132]{0,1:T(8,128)(2,1)S(1)} %maximum_select_fusion.3), channel_id=1, source_target_pairs={{0,8},{2,10},{4,12},{6,14},{8,0},{10,2},{12,4},{14,6},{16,24},{18,... | collective-permute-start | bytes 811016 | tf_op jit(solution)/shard_map/ppermute | solution.py:145
  21.1 1.4 copy-start.24
  21.4 31.2 %copy-start.7 = (bf16[1,128,2176]{1,2,0:T(8,128)(2,1)}, bf16[1,128,2176]{1,2,0:T(8,128)(2,1)S(1)}, u32[]{:S(2)}) copy-start(bf16[1,128,2176]{1,2,0:T(8,128)(2,1)S(1)} %copy.78) | copy-start | bytes 1671172
  21.5 8.9 %copy-start.26 = (f32[68]{0:T(128)S(1)}, f32[68]{0:T(128)}, u32[]{:S(2)}) copy-start(f32[68]{0:T(128)} %param.16) | copy-start | bytes 820
  21.5 8.9 %copy-start.8 = (bf16[1,128,64]{1,2,0:T(8,128)(2,1)S(1)}, bf16[1,128,64]{1,2,0:T(8,128)(2,1)}, u32[]{:S(2)}) copy-start(bf16[1,128,64]{1,2,0:T(8,128)(2,1)} %param.14) | copy-start | bytes 49156
  25.8 24.2 %collective-permute-start.3 = (bf16[2048,132]{0,1:T(8,128)(2,1)S(1)}, bf16[2048,132]{0,1:T(8,128)(2,1)S(1)}, u32[]{:S(2)}, u32[]{:S(2)}) collective-permute-start(bf16[2048,132]{0,1:T(8,128)(2,1)S(1)} %maximum_select_fusion.2), channel_id=1, source_target_pairs={{0,16},{2,18},{4,20},{6,22},{8,24},{10,26},{12,28},{14,30},{16,0},... | collective-permute-start | bytes 1622024 | tf_op jit(solution)/shard_map/ppermute | solution.py:145
  30.4 20.2 %copy-start.23 = (f32[68]{0:T(128)}, f32[68]{0:T(128)S(1)}, u32[]{:S(2)}) copy-start(f32[68]{0:T(128)S(1)} %exponential_negate_fusion) | copy-start | bytes 820
  31.0 19.5 %copy-start.21 = (f32[68]{0:T(128)S(1)}, f32[68]{0:T(128)}, u32[]{:S(2)}) copy-start(f32[68]{0:T(128)} %param.17) | copy-start | bytes 820
  52.5 3.4 %copy-start.12 = (f32[68,128]{1,0:T(8,128)}, f32[68,128]{1,0:T(8,128)S(1)}, u32[]{:S(2)}) copy-start(f32[68,128]{1,0:T(8,128)S(1)} %copy.71) | copy-start | bytes 104452
  52.6 3.3 %copy-start.15 = (f32[128,64]{0,1:T(8,128)}, f32[128,64]{0,1:T(8,128)S(1)}, u32[]{:S(2)}) copy-start(f32[128,64]{0,1:T(8,128)S(1)} %copy.68) | copy-start | bytes 98308
  61.4 3.6 %copy-start.27 = (bf16[2,68]{1,0:T(2,128)(2,1)S(1)}, bf16[2,68]{1,0:T(2,128)(2,1)}, u32[]{:S(2)}) copy-start(bf16[2,68]{1,0:T(2,128)(2,1)} %get-tuple-element.694) | copy-start | bytes 820
  65.0 1.6 copy-start.13
  68.9 1.1 copy-start.1
  99.6 1.0 copy-start.3
  102.6 0.8 copy-start.9
  105.3 2.0 %copy-start.17 = (bf16[128,128]{1,0:T(8,128)(2,1)S(1)}, bf16[128,128]{1,0:T(8,128)(2,1)}, u32[]{:S(2)}) copy-start(bf16[128,128]{1,0:T(8,128)(2,1)} %get-tuple-element.538) | copy-start | bytes 98308
  105.3 2.9 %copy-start.2 = (bf16[1,128,2176]{1,2,0:T(8,128)(2,1)S(1)}, bf16[1,128,2176]{1,2,0:T(8,128)(2,1)}, u32[]{:S(2)}) copy-start(bf16[1,128,2176]{1,2,0:T(8,128)(2,1)} %copy.65) | copy-start | bytes 1671172
  105.3 2.8 %copy-start.11 = (f32[1,68,128]{2,1,0:T(8,128)S(1)}, f32[1,68,128]{2,1,0:T(8,128)}, u32[]{:S(2)}) copy-start(f32[1,68,128]{2,1,0:T(8,128)} %copy-done.10) | copy-start | bytes 104452
  105.3 2.8 %copy-start.18 = (f32[128,128]{1,0:T(8,128)S(1)}, f32[128,128]{1,0:T(8,128)}, u32[]{:S(2)}) copy-start(f32[128,128]{1,0:T(8,128)} %copy.72) | copy-start | bytes 196612
  105.3 2.8 %copy-start.19 = (f32[68,128]{1,0:T(8,128)S(1)}, f32[68,128]{1,0:T(8,128)}, u32[]{:S(2)}) copy-start(f32[68,128]{1,0:T(8,128)} %copy.75) | copy-start | bytes 104452
  105.3 2.8 %copy-start.20 = (pred[128,128]{1,0:T(8,128)(4,1)S(1)}, pred[128,128]{1,0:T(8,128)(4,1)}, u32[]{:S(2)}) copy-start(pred[128,128]{1,0:T(8,128)(4,1)} %iota_compare_fusion) | copy-start | bytes 49156
  108.1 2.0 %copy-start.14 = (f32[68,128]{1,0:T(8,128)S(1)}, f32[68,128]{1,0:T(8,128)}, u32[]{:S(2)}) copy-start(f32[68,128]{1,0:T(8,128)} %copy-done.12) | copy-start | bytes 104452
  108.2 2.0 %copy-start.16 = (f32[128,64]{0,1:T(8,128)S(1)}, f32[128,64]{0,1:T(8,128)}, u32[]{:S(2)}) copy-start(f32[128,64]{0,1:T(8,128)} %copy-done.15) | copy-start | bytes 98308
  108.2 2.0 %copy-start.25 = (f32[68]{0:T(128)S(1)}, f32[68]{0:T(128)}, u32[]{:S(2)}) copy-start(f32[68]{0:T(128)} %param.18) | copy-start | bytes 820
  110.2 80.4 %copy-start.4 = (f32[128,68]{1,0:T(8,128)S(1)}, f32[128,68]{1,0:T(8,128)}, u32[]{:S(2)}) copy-start(f32[128,68]{1,0:T(8,128)} %copy-done.3) | copy-start | bytes 104452
  188.3 4.2 %collective-permute-start.4 = (f32[256,6]{0,1:T(8,128)S(1)}, f32[256,6]{0,1:T(8,128)S(1)}, u32[]{:S(2)}, u32[]{:S(2)}) collective-permute-start(f32[256,6]{0,1:T(8,128)S(1)} %slice.28), channel_id=1, source_target_pairs={{0,1},{2,3},{4,5},{6,7},{8,9},{10,11},{12,13},{14,15},{16,17},{18,... | collective-permute-start | bytes 18440
  (2 other events, 1.4 us)
Sparse Core Ops, SparseCore 0:
  102.7 81.8 reduce-scatter.3
